TPU v7x, 32 devices: a whole 2x2x4 slice. The times are simulated.
32 devices in a mesh: tm: 8 (over z, y), roll: 4 (over x, core).
Axes of the slice: x: 2, y: 2, z: 4, core: 2. Of those that a mesh axis runs over, the one named last changes fastest.
Arguments:
- inputs: bfloat16 [4, 64, 32, 2048], P('roll', 'tm'), may hold values from -30 to 30
- cotangent: bfloat16 [4, 64, 32, 2048], P('roll', 'tm'), may hold values from -6 to 6
- memory_lists: int32 [4, 64, 8], P('roll', 'tm'), may hold values from -1 to 55, as said below
- w_query: bfloat16 [2048, 1024], replicated, may hold values from -1 to 1
- w_key: bfloat16 [2048, 1024], replicated, may hold values from -1 to 1
- w_value: bfloat16 [2048, 1024], replicated, may hold values from -0.125 to 0.125
- w_output: bfloat16 [1024, 2048], replicated, may hold values from -0.1875 to 0.1875
Outputs:
- attended: bfloat16 [4, 64, 32, 2048], P('roll', 'tm')
- grad_input: bfloat16 [4, 64, 32, 2048], P('roll', 'tm')
- grad_w_query: float32 [2048, 1024], P('tm')
- grad_w_key: float32 [2048, 1024], P('tm')
- grad_w_value: float32 [2048, 1024], P('tm')
- grad_w_output: float32 [1024, 2048], P('tm')
Inputs may be any that keep to these rules, and one draw needn't show every extreme that they name: `memory_lists`: every entry is -1 or a frame of the same rollout that lies in an earlier block of 8 frames and before frame f - 4. The frames named in one list differ, and -1 entries come after them. The frames of one block name at most 3 distinct frames of any other block, and exactly 3 of the block just before theirs.
All inputs are finite; a program needn't handle non-finite values.
Results may differ from a plain program's by a relative error of at most 0.02.
Values may be sent and summed in bfloat16 or wider, within the bound.
A program may use at most 192 MiB of HBM per device.

v0:
```python
import jax
import jax.numpy as jnp
from jax import lax
from jax.sharding import PartitionSpec as P

HEADS = 8
HEAD = 128
BAND = 4
MEM = 8
CAP = 3
masked_score = -1e30


def from_behind(block, axis, distance):
    devices = range(lax.axis_size(axis))
    route = [(i - distance, i) for i in devices if i - distance in devices]
    return lax.ppermute(block, axis, route)


def dot_last(left, right):
    return lax.dot_general(
        left, right, (((1,), (1,)), ((), ())), preferred_element_type=jnp.float32
    )


def dot_first(left, right):
    return lax.dot_general(
        left, right, (((0,), (0,)), ((), ())), preferred_element_type=jnp.float32
    )


def attend(queries, key_set, value_set, key_valid, grad_heads):
    frame_count, key_count, frame_tokens, inner_width = key_set.shape
    score_scale = HEAD ** (-0.5)
    query_h = queries.reshape(frame_count, frame_tokens, HEADS, HEAD)
    key_h = key_set.reshape(frame_count, key_count * frame_tokens, HEADS, HEAD)
    value_h = value_set.reshape(frame_count, key_count * frame_tokens, HEADS, HEAD)
    grad_h = grad_heads.reshape(frame_count, frame_tokens, HEADS, HEAD)
    scores = (
        jnp.einsum("fqhe,fkhe->fhqk", query_h, key_h, preferred_element_type=jnp.float32)
        * score_scale
    )
    key_mask = jnp.repeat(key_valid, frame_tokens, axis=1)[:, None, None, :]
    scores = jnp.where(key_mask, scores, masked_score)
    row_max = jnp.max(scores, axis=-1, keepdims=True)
    weights = jnp.exp(scores - row_max)
    weights = weights / jnp.sum(weights, axis=-1, keepdims=True)
    rounded = weights.astype(jnp.bfloat16)
    heads_out = jnp.einsum(
        "fhqk,fkhe->fqhe", rounded, value_h, preferred_element_type=jnp.float32
    ).astype(jnp.bfloat16)
    grad_prob = jnp.einsum("fqhe,fkhe->fhqk", grad_h, value_h, preferred_element_type=jnp.float32)
    row_dot = jnp.sum(weights * grad_prob, axis=-1, keepdims=True)
    dscore = (weights * (grad_prob - row_dot)).astype(jnp.bfloat16)
    grad_query = (
        jnp.einsum("fhqk,fkhe->fqhe", dscore, key_h, preferred_element_type=jnp.float32)
        * score_scale
    ).astype(jnp.bfloat16)
    grad_keys = (
        jnp.einsum("fhqk,fqhe->fkhe", dscore, query_h, preferred_element_type=jnp.float32)
        * score_scale
    )
    grad_values = jnp.einsum("fhqk,fqhe->fkhe", rounded, grad_h, preferred_element_type=jnp.float32)
    block_shape = (frame_count, key_count, frame_tokens, inner_width)
    return (
        heads_out.reshape(frame_count, frame_tokens, inner_width),
        grad_query.reshape(frame_count, frame_tokens, inner_width),
        grad_keys.reshape(block_shape),
        grad_values.reshape(block_shape),
    )


def spread_band(grad_band):
    frame_count, unused, frame_tokens, inner_width = grad_band.shape
    spread = jnp.zeros((frame_count + BAND, frame_tokens, inner_width), jnp.float32)
    for offset in range(BAND + 1):
        spread = spread + jnp.pad(grad_band[:, offset], ((offset, BAND - offset), (0, 0), (0, 0)))
    return spread


def slot_sum(hit_matrix, part):
    flat = part.reshape(part.shape[0] * part.shape[1], -1)
    high = flat.astype(jnp.bfloat16)
    low = (flat - high.astype(jnp.float32)).astype(jnp.bfloat16)
    return dot_first(hit_matrix, high) + dot_first(hit_matrix, low)


def local(inputs, cotangent, memory_lists, w_query, w_key, w_value, w_output):
    frame_count, frame_tokens, model_width = inputs.shape[1:]
    inner_width = w_query.shape[1]
    blocks = lax.axis_size("tm")
    position = lax.axis_index("tm")
    row_count = frame_count * frame_tokens
    flat_input = inputs.reshape(row_count, model_width)
    grad_flat = cotangent.reshape(row_count, model_width)
    queries = jnp.dot(flat_input, w_query, preferred_element_type=jnp.float32).astype(jnp.bfloat16)
    key_rows = jnp.dot(flat_input, w_key, preferred_element_type=jnp.float32).astype(jnp.bfloat16)
    value_rows = jnp.dot(flat_input, w_value, preferred_element_type=jnp.float32).astype(
        jnp.bfloat16
    )
    key_frames = key_rows.reshape(frame_count, frame_tokens, inner_width)
    value_frames = value_rows.reshape(frame_count, frame_tokens, inner_width)
    grad_heads = dot_last(grad_flat, w_output).astype(jnp.bfloat16)
    recalled = memory_lists[0]
    first_frame = position * frame_count
    last_frames = jnp.concatenate(
        [key_frames[frame_count - BAND :], value_frames[frame_count - BAND :]], axis=-1
    )
    before = from_behind(last_frames, "tm", 1)
    extended_keys = jnp.concatenate([before[..., :inner_width], key_frames], axis=0)
    extended_values = jnp.concatenate([before[..., inner_width:], value_frames], axis=0)
    band_keys = jnp.stack(
        [extended_keys[offset : offset + frame_count] for offset in range(BAND + 1)], axis=1
    )
    band_values = jnp.stack(
        [extended_values[offset : offset + frame_count] for offset in range(BAND + 1)], axis=1
    )
    band_index = (
        jnp.arange(frame_count, dtype=jnp.int32)[:, None]
        + jnp.arange(BAND + 1, dtype=jnp.int32)[None, :]
    )
    band_ok = first_frame + band_index - BAND >= 0
    all_lists = lax.all_gather(recalled, "tm", axis=0, tiled=True)
    targets = jnp.arange(blocks * frame_count, dtype=jnp.int32)
    wanted = jnp.any(recalled.reshape(-1, 1) == targets[None, :], axis=0).reshape(
        blocks, frame_count
    )
    slot_rank = jnp.cumsum(wanted.astype(jnp.int32), axis=1) - 1
    slot_table = (jnp.arange(blocks, dtype=jnp.int32)[:, None] * CAP + slot_rank).reshape(-1)
    mem_ok = recalled >= 0
    safe_ids = jnp.where(mem_ok, recalled, 0)
    slot_ids = jnp.where(mem_ok, slot_table[safe_ids], 0)
    own_frames = first_frame + jnp.arange(frame_count, dtype=jnp.int32)
    requested = jnp.any(
        all_lists.reshape(blocks, frame_count * MEM, 1) == own_frames[None, None, :], axis=1
    )
    asked_rank = jnp.cumsum(requested.astype(jnp.int32), axis=1) - 1
    picker = requested[:, None, :] & (
        asked_rank[:, None, :] == jnp.arange(CAP, dtype=jnp.int32)[None, :, None]
    )
    picker = picker.astype(jnp.bfloat16)
    out_keys = jnp.einsum(
        "bcp,pz->bcz", picker, key_rows.reshape(frame_count, -1), preferred_element_type=jnp.float32
    )
    out_values = jnp.einsum(
        "bcp,pz->bcz",
        picker,
        value_rows.reshape(frame_count, -1),
        preferred_element_type=jnp.float32,
    )
    piece_shape = (blocks, CAP, frame_tokens, inner_width)
    outgoing = jnp.concatenate(
        [
            out_keys.astype(jnp.bfloat16).reshape(piece_shape),
            out_values.astype(jnp.bfloat16).reshape(piece_shape),
        ],
        axis=-1,
    )
    incoming = lax.all_to_all(outgoing, "tm", split_axis=0, concat_axis=0, tiled=True)
    slot_rows = incoming.reshape(blocks * CAP, frame_tokens, 2 * inner_width)
    memory_keys = slot_rows[..., :inner_width][slot_ids]
    memory_values = slot_rows[..., inner_width:][slot_ids]
    key_set = jnp.concatenate([band_keys, memory_keys], axis=1)
    value_set = jnp.concatenate([band_values, memory_values], axis=1)
    key_valid = jnp.concatenate([band_ok, mem_ok], axis=1)
    heads_out, grad_query, grad_keys_all, grad_values_all = attend(
        queries.reshape(frame_count, frame_tokens, inner_width),
        key_set,
        value_set,
        key_valid,
        grad_heads.reshape(frame_count, frame_tokens, inner_width),
    )
    key_spread = spread_band(grad_keys_all[:, : BAND + 1])
    value_spread = spread_band(grad_values_all[:, : BAND + 1])
    rim = jnp.concatenate([key_spread[:BAND], value_spread[:BAND]], axis=-1).astype(jnp.bfloat16)
    passed = from_behind(rim, "tm", -1)
    passed_full = jnp.pad(passed.astype(jnp.float32), ((frame_count - BAND, 0), (0, 0), (0, 0)))
    slot_hits = (
        slot_ids.reshape(-1, 1) == jnp.arange(blocks * CAP, dtype=jnp.int32)[None, :]
    ) & mem_ok.reshape(-1, 1)
    hit_matrix = slot_hits.astype(jnp.bfloat16)
    slot_keys = (
        slot_sum(hit_matrix, grad_keys_all[:, BAND + 1 :]).astype(jnp.bfloat16).reshape(piece_shape)
    )
    slot_values = (
        slot_sum(hit_matrix, grad_values_all[:, BAND + 1 :])
        .astype(jnp.bfloat16)
        .reshape(piece_shape)
    )
    slot_grad = jnp.concatenate([slot_keys, slot_values], axis=-1)
    returned = lax.all_to_all(slot_grad, "tm", split_axis=0, concat_axis=0, tiled=True)
    gathered_back = jnp.einsum(
        "bcp,bcz->pz", picker, returned.reshape(blocks, CAP, -1), preferred_element_type=jnp.float32
    )
    gathered_back = gathered_back.reshape(frame_count, frame_tokens, 2 * inner_width)
    grad_keys = (
        key_spread[BAND:] + passed_full[..., :inner_width] + gathered_back[..., :inner_width]
    ).astype(jnp.bfloat16)
    grad_values = (
        value_spread[BAND:] + passed_full[..., inner_width:] + gathered_back[..., inner_width:]
    ).astype(jnp.bfloat16)
    grad_keys = grad_keys.reshape(row_count, inner_width)
    grad_values = grad_values.reshape(row_count, inner_width)
    query_rows = grad_query.reshape(row_count, inner_width)
    heads_rows = heads_out.reshape(row_count, inner_width)
    grad_input = (
        dot_last(query_rows, w_query) + dot_last(grad_keys, w_key) + dot_last(grad_values, w_value)
    )
    grad_input = grad_input.astype(jnp.bfloat16).reshape(1, frame_count, frame_tokens, model_width)
    attended = jnp.dot(heads_rows, w_output, preferred_element_type=jnp.float32).astype(
        jnp.bfloat16
    )
    attended = attended.reshape(1, frame_count, frame_tokens, model_width)
    partials = (
        dot_first(flat_input, query_rows).astype(jnp.bfloat16),
        dot_first(flat_input, grad_keys).astype(jnp.bfloat16),
        dot_first(flat_input, grad_values).astype(jnp.bfloat16),
        dot_first(heads_rows, grad_flat).astype(jnp.bfloat16),
    )
    shares = (
        lax.psum_scatter(partials[0], "tm", scatter_dimension=0, tiled=True).astype(jnp.float32),
        lax.psum_scatter(partials[1], "tm", scatter_dimension=0, tiled=True).astype(jnp.float32),
        lax.psum_scatter(partials[2], "tm", scatter_dimension=0, tiled=True).astype(jnp.float32),
        lax.psum_scatter(partials[3], "tm", scatter_dimension=0, tiled=True).astype(jnp.float32),
    )
    totals = (
        lax.psum(shares[0].astype(jnp.bfloat16), "roll").astype(jnp.float32),
        lax.psum(shares[1].astype(jnp.bfloat16), "roll").astype(jnp.float32),
        lax.psum(shares[2].astype(jnp.bfloat16), "roll").astype(jnp.float32),
        lax.psum(shares[3].astype(jnp.bfloat16), "roll").astype(jnp.float32),
    )
    return (attended, grad_input, totals[0], totals[1], totals[2], totals[3])


def solution(mesh):
    return jax.shard_map(
        local,
        mesh=mesh,
        in_specs=(
            P("roll", "tm", None, None),
            P("roll", "tm", None, None),
            P("roll", "tm", None),
            P(),
            P(),
            P(),
            P(),
        ),
        out_specs=(
            P("roll", "tm", None, None),
            P("roll", "tm", None, None),
            P("tm", None),
            P("tm", None),
            P("tm", None),
            P("tm", None),
        ),
        check_vma=False,
    )
```

profile of v0, /device:TPU:0, one launch (start us, length us, event | category | flops | bytes accessed | tf_op | source)
XLA Modules:
  0.0 683.3 jit_solution(1070487191711943485)
XLA Ops:
  7.2 32.7 %all-gather = s32[1,64,8]{2,1,0:T(8,128)S(1)} all-gather(s32[1,8,8]{2,1,0:T(8,128)} %param.9), channel_id=2, replica_groups=mesh['tm'=8,'roll'=4] {'tm'}, dimensions={1}, use_global_device_ids=true | all-gather | bytes 2304 | tf_op jit(solution)/shard_map/all_gather | solution.py:123
  50.9 5.6 all-to-all-start
  57.5 4.8 collective-permute-start
  70.2 19.8 %collective-permute-done = bf16[4,32,2048]{2,1,0:T(8,128)(2,1)} collective-permute-done((bf16[4,32,2048]{2,1,0:T(8,128)(2,1)}, bf16[4,32,2048]{2,1,0:T(8,128)(2,1)}, u32[]{:S(2)}, u32[]{:S(2)}) %collective-permute-start) | collective-permute-done | bytes 524320 | tf_op jit(solution)/shard_map/ppermute | solution.py:17
  99.3 21.9 %all-to-all-done = bf16[8,3,32,2048]{3,2,1,0:T(8,128)(2,1)} async-done(((bf16[8,3,32,2048]{3,2,1,0:T(8,128)(2,1)}), bf16[8,3,32,2048]{3,2,1,0:T(8,128)(2,1)}, u32[]{:S(2)}, u32[]{:S(2)}) %all-to-all-start) | async-done | bytes 3145760 | tf_op jit(solution)/shard_map/all_to_all | solution.py:159
  131.7 5.0 constant_dynamic-update-slice_fusion.2
  136.7 4.9 copy.180
  144.4 5.5 copy.179
  168.1 5.8 fusion.42
  174.9 7.0 %convolution_bitcast_fusion = f32[8,416,8,128]{3,1,2,0:T(8,128)} fusion(bf16[8,32,8,128]{3,2,1,0:T(8,128)(2,1)S(1)} %bitcast.264, f32[8,8,32,416]{3,2,1,0:T(8,128)S(1)} %copy-done.3, f32[8,8,32]{2,1,0:T(8,128)S(1)} %get-tuple-element.50), kind=kOutput, calls=%fused_computation.15 | convolution fusion | flops 219807744 | bytes 17571840 | tf_op jit(solution)/shard_map/fhqk,fqhe->fkhe/dot_general | solution.py:63
  181.9 17.5 %copy.151 = f32[8,416,8,128]{3,2,1,0:T(8,128)} copy(f32[8,416,8,128]{3,1,2,0:T(8,128)} %convolution_bitcast_fusion) | data formatting | bytes 27262976 | tf_op jit(solution)/shard_map/fhqk,fqhe->fkhe/transpose | solution.py:63
  199.4 15.8 %reshape.193 = f32[8,13,32,1024]{3,2,1,0:T(8,128)} reshape(f32[8,416,8,128]{3,2,1,0:T(8,128)} %copy.151) | data formatting | bytes 27262976 | tf_op jit(solution)/shard_map/reshape | solution.py:69
  219.4 5.0 copy.186
  228.3 6.3 multiply_bitcast_fusion
  234.6 17.5 %copy.144 = f32[8,416,8,128]{3,2,1,0:T(8,128)} copy(f32[8,416,8,128]{3,1,2,0:T(8,128)} %multiply_bitcast_fusion) | data formatting | bytes 27262976 | tf_op jit(solution)/shard_map/mul | solution.py:60
  252.1 16.0 %reshape.192 = f32[8,13,32,1024]{3,2,1,0:T(8,128)} reshape(f32[8,416,8,128]{3,2,1,0:T(8,128)} %copy.144) | data formatting | bytes 27262976 | tf_op jit(solution)/shard_map/reshape | solution.py:68
  275.9 5.0 copy.184
  286.1 23.4 %all-to-all-start.1 = ((bf16[8,3,32,2048]{3,2,1,0:T(8,128)(2,1)}), bf16[8,3,32,2048]{3,2,1,0:T(8,128)(2,1)}, u32[]{:S(2)}, u32[]{:S(2)}) async-start(bf16[8,3,32,2048]{3,2,1,0:T(8,128)(2,1)} %pad_maximum_fusion.1), calls=%async_computation.1 | async-start | bytes 6291456 | tf_op jit(solution)/shard_map/all_to_all | solution.py:191
  327.6 21.7 %collective-permute-done.1 = bf16[4,32,2048]{2,0,1:T(4,128)(2,1)S(1)} collective-permute-done((bf16[4,32,2048]{2,0,1:T(4,128)(2,1)S(1)}, bf16[4,32,2048]{2,0,1:T(4,128)(2,1)S(1)}, u32[]{:S(2)}, u32[]{:S(2)}) %collective-permute-start.1) | collective-permute-done | bytes 524320 | tf_op jit(solution)/shard_map/ppermute | solution.py:17
  349.6 52.4 %all-to-all-done.1 = bf16[8,3,32,2048]{3,2,1,0:T(8,128)(2,1)} async-done(((bf16[8,3,32,2048]{3,2,1,0:T(8,128)(2,1)}), bf16[8,3,32,2048]{3,2,1,0:T(8,128)(2,1)}, u32[]{:S(2)}, u32[]{:S(2)}) %all-to-all-start.1) | async-done | bytes 3145760 | tf_op jit(solution)/shard_map/all_to_all | solution.py:191
  406.0 5.2 reshape.198
  431.0 92.4 %reduce-scatter.9.cloned.1.call-done = bf16[256,1024]{0,1:T(8,128)(2,1)} async-done(((bf16[2048,1024]{0,1:T(8,128)(2,1)}), bf16[256,1024]{0,1:T(8,128)(2,1)}) %reduce-scatter.9.cloned.1.call-update) | async-done | bytes 524304 | tf_op jit(solution)/shard_map/reduce_scatter | solution.py:223
  523.4 91.8 %reduce-scatter.7.cloned.1.call-done = bf16[256,1024]{0,1:T(8,128)(2,1)} async-done(((bf16[2048,1024]{0,1:T(8,128)(2,1)}), bf16[256,1024]{0,1:T(8,128)(2,1)}) %reduce-scatter.7.cloned.1.call-update) | async-done | bytes 524304 | tf_op jit(solution)/shard_map/reduce_scatter | solution.py:222
  623.4 45.4 %all-reduce.14.cloned.1.call-done = (bf16[256,1024]{0,1:T(8,128)(2,1)}, bf16[256,1024]{0,1:T(8,128)(2,1)}, bf16[256,1024]{0,1:T(8,128)(2,1)}, bf16[128,2048]{1,0:T(8,128)(2,1)}) async-done(((bf16[256,1024]{0,1:T(8,128)(2,1)}, bf16[256,1024]{0,1:T(8,128)(2,1)}, bf16[256,1024]{0,1:T(8,128)(2,1)}, bf16[128,2048]{1,0:T(8,128)(2,1)}), (bf16[256,1024]{0,1:T(8,128)(2,1)}, bf16[256,1024]{0,1:T(8,128)(2,1)}, ...) | async-done | bytes 2097168 | tf_op jit(solution)/shard_map/psum | solution.py:227
  (187 shorter events, 140.1 us)
Async XLA Ops:
  7.2 33.4 %copy-start = (bf16[1,8,32,2048]{3,2,1,0:T(8,128)(2,1)S(1)}, bf16[1,8,32,2048]{3,2,1,0:T(8,128)(2,1)}, u32[]{:S(2)}) copy-start(bf16[1,8,32,2048]{3,2,1,0:T(8,128)(2,1)} %param.7) | copy-start | bytes 3145732
  40.3 7.2 %copy-start.27 = (pred[8,8]{0,1:T(8,128)(4,1)}, pred[8,8]{0,1:T(8,128)(4,1)S(1)}, u32[]{:S(2)}) copy-start(pred[8,8]{0,1:T(8,128)(4,1)S(1)} %copy.121) | copy-start | bytes 196
  40.6 6.9 %copy-start.25 = (s32[8,8]{0,1:T(8,128)}, s32[8,8]{0,1:T(8,128)S(1)}, u32[]{:S(2)}) copy-start(s32[8,8]{0,1:T(8,128)S(1)} %copy.122) | copy-start | bytes 772
  50.9 11.4 %copy-start.24 = (s32[1,8,8]{2,1,0:T(8,128)S(1)}, s32[1,8,8]{2,1,0:T(8,128)}, u32[]{:S(2)}) copy-start(s32[1,8,8]{2,1,0:T(8,128)} %param.9) | copy-start | bytes 772
  50.9 70.3 %all-to-all-start = ((bf16[8,3,32,2048]{3,2,1,0:T(8,128)(2,1)}), bf16[8,3,32,2048]{3,2,1,0:T(8,128)(2,1)}, u32[]{:S(2)}, u32[]{:S(2)}) async-start(bf16[8,3,32,2048]{3,2,1,0:T(8,128)(2,1)} %pad_maximum_fusion), calls=%async_computation | async-start | bytes 6291456 | tf_op jit(solution)/shard_map/all_to_all | solution.py:159
  56.6 371.5 %reduce-scatter.5.cloned.1.call-start = ((), (), s32[]{:S(2)}) async-start(), calls=%async_computation.6 | async-start | bytes 4718592 | tf_op jit(solution)/shard_map/reduce_scatter | solution.py:221
  57.5 32.6 %collective-permute-start = (bf16[4,32,2048]{2,1,0:T(8,128)(2,1)}, bf16[4,32,2048]{2,1,0:T(8,128)(2,1)}, u32[]{:S(2)}, u32[]{:S(2)}) collective-permute-start(bf16[4,32,2048]{2,1,0:T(8,128)(2,1)} %pad_maximum_fusion.4), channel_id=1, source_target_pairs={{0,4},{4,8},{8,12},{12,16},{16,20},{20,24},{24,28},{1,5},{5,9},{9,... | collective-permute-start | bytes 1572872 | tf_op jit(solution)/shard_map/ppermute | solution.py:17
  68.0 81.9 %copy-start.10 = (bf16[32,8,8,128]{3,2,1,0:T(8,128)(2,1)}, bf16[32,8,8,128]{3,2,1,0:T(8,128)(2,1)S(1)}, u32[]{:S(2)}) copy-start(bf16[32,8,8,128]{3,2,1,0:T(8,128)(2,1)S(1)} %copy.178) | copy-start | bytes 1572868
  136.7 4.9 copy-start.1
  141.6 13.5 %copy-start.4 = (bf16[416,8,8,128]{3,2,1,0:T(8,128)(2,1)}, bf16[416,8,8,128]{3,2,1,0:T(8,128)(2,1)S(1)}, u32[]{:S(2)}) copy-start(bf16[416,8,8,128]{3,2,1,0:T(8,128)(2,1)S(1)} %copy.180) | copy-start | bytes 20447236
  168.0 263.0 %reduce-scatter.11.cloned.1.call-start = ((), (), s32[]{:S(2)}) async-start(), calls=%async_computation.9 | async-start | bytes 4718592 | tf_op jit(solution)/shard_map/reduce_scatter | solution.py:224
  168.0 6.9 %copy-start.3 = (f32[8,8,32,416]{3,2,1,0:T(8,128)S(1)}, f32[8,8,32,416]{3,2,1,0:T(8,128)}, u32[]{:S(2)}) copy-start(f32[8,8,32,416]{3,2,1,0:T(8,128)} %copy-done.2) | copy-start | bytes 10223620
  168.1 6.9 %copy-start.20 = (bf16[32,8,8,128]{3,2,1,0:T(8,128)(2,1)S(1)}, bf16[32,8,8,128]{3,2,1,0:T(8,128)(2,1)}, u32[]{:S(2)}) copy-start(bf16[32,8,8,128]{3,2,1,0:T(8,128)(2,1)} %copy.182) | copy-start | bytes 1572868
  252.1 16.1 %copy-start.16 = (bf16[8,32,8,128]{3,2,1,0:T(8,128)(2,1)S(1)}, bf16[8,32,8,128]{3,2,1,0:T(8,128)(2,1)}, u32[]{:S(2)}) copy-start(bf16[8,32,8,128]{3,2,1,0:T(8,128)(2,1)} %copy.138) | copy-start | bytes 1572868
  252.1 16.1 %copy-start.22 = (bf16[1,8,32,2048]{3,2,1,0:T(8,128)(2,1)S(1)}, bf16[1,8,32,2048]{3,2,1,0:T(8,128)(2,1)}, u32[]{:S(2)}) copy-start(bf16[1,8,32,2048]{3,2,1,0:T(8,128)(2,1)} %param.8) | copy-start | bytes 3145732
  286.1 115.9 %all-to-all-start.1 = ((bf16[8,3,32,2048]{3,2,1,0:T(8,128)(2,1)}), bf16[8,3,32,2048]{3,2,1,0:T(8,128)(2,1)}, u32[]{:S(2)}, u32[]{:S(2)}) async-start(bf16[8,3,32,2048]{3,2,1,0:T(8,128)(2,1)} %pad_maximum_fusion.1), calls=%async_computation.1 | async-start | bytes 6291456 | tf_op jit(solution)/shard_map/all_to_all | solution.py:191
  309.5 214.0 %reduce-scatter.9.cloned.1.call-start = ((), (), s32[]{:S(2)}) async-start(), calls=%async_computation.8 | async-start | bytes 4718592 | tf_op jit(solution)/shard_map/reduce_scatter | solution.py:223
  326.1 23.2 %collective-permute-start.1 = (bf16[4,32,2048]{2,0,1:T(4,128)(2,1)S(1)}, bf16[4,32,2048]{2,0,1:T(4,128)(2,1)S(1)}, u32[]{:S(2)}, u32[]{:S(2)}) collective-permute-start(bf16[4,32,2048]{2,0,1:T(4,128)(2,1)S(1)} %pad_maximum_fusion.5), channel_id=1, source_target_pairs={{4,0},{8,4},{12,8},{16,12},{20,16},{24,20},{28,24},{5,1},{9,5},{13... | collective-permute-start | bytes 1572872 | tf_op jit(solution)/shard_map/ppermute | solution.py:17
  406.0 5.2 copy-start.26
  406.0 5.2 copy-start.28
  419.7 195.5 %reduce-scatter.7.cloned.1.call-start = ((), (), s32[]{:S(2)}) async-start(), calls=%async_computation.7 | async-start | bytes 4718592 | tf_op jit(solution)/shard_map/reduce_scatter | solution.py:222
  423.4 191.9 %copy-start.15 = (bf16[8,32,8,128]{3,2,1,0:T(8,128)(2,1)S(1)}, bf16[8,32,8,128]{3,2,1,0:T(8,128)(2,1)}, u32[]{:S(2)}) copy-start(bf16[8,32,8,128]{3,2,1,0:T(8,128)(2,1)} %copy-done.14) | copy-start | bytes 1572868
  423.4 245.3 %all-reduce.14.cloned.1.call-start = ((), (), s32[]{:S(2)}) async-start(), calls=%async_computation.10 | async-start | bytes 4194304 | tf_op jit(solution)/shard_map/psum | solution.py:227
  668.8 6.7 copy-start.23
  (16 other events, 45.0 us)
Sparse Core Ops, SparseCore 0:
  168.1 107.1 reduce-scatter.4
  278.9 152.0 reduce-scatter.10
  434.6 88.7 reduce-scatter.8
  526.9 88.3 reduce-scatter.6
  617.7 51.0 all-reduce.13
where the time goes:
time: 690 us; the launch traced here: 683 us
  waiting for transfers between devices  348 us (50%)
  local copies, waits for them, and re-layouts  159 us (23%)
  matrix products  69.8 us (10%)
  starting transfers between devices  35.7 us (5%)
  blocking collectives  32.7 us (5%)
  other arithmetic  22.6 us (3%)
  between operations  14.8 us (2%)
    reduce_scatter x1, waiting for transfers between devices, local(): lax.psum_scatter(partials[2], 'tm', scatter_dimension=0, tiled=True)  92.4 us
    reduce_scatter x1, waiting for transfers between devices, local(): lax.psum_scatter(partials[1], 'tm', scatter_dimension=0, tiled=True)  91.8 us
    all_to_all x1, waiting for transfers between devices, local(): lax.all_to_all(slot_grad, 'tm', split_axis=0, concat_axis=0, tiled=True)  52.4 us
    unnamed x87, local copies, waits for them, and re-layouts  51.6 us
    psum x1, waiting for transfers between devices, local(): lax.psum(shares[0].astype(jnp.bfloat16), 'roll').astype(jnp.float32)  45.4 us
    ppermute x2, waiting for transfers between devices, from_behind(): return lax.ppermute(block, axis, route)  41.5 us
    all_gather x1, blocking collectives, local(): all_lists = lax.all_gather(recalled, 'tm', axis=0, tiled=True)  32.7 us
    all_to_all x1, starting transfers between devices, local(): lax.all_to_all(slot_grad, 'tm', split_axis=0, concat_axis=0, tiled=True)  23.4 us
  transfers between devices with their start and end apart: 9, of which 8 were waited for; matrix products, arithmetic and copies ran while one was open for 27% of the time, Pallas kernels for 0%

commit v1 on v0

--- a/solution.py
+++ b/solution.py
@@ -224,7 +224,7 @@
         lax.psum_scatter(partials[3], "tm", scatter_dimension=0, tiled=True).astype(jnp.float32),
     )
     totals = (
-        lax.psum(shares[0].astype(jnp.bfloat16), "roll").astype(jnp.float32),
+        jnp.sum(lax.all_gather(shares[0].astype(jnp.bfloat16), "roll"), axis=0).astype(jnp.float32),
         lax.psum(shares[1].astype(jnp.bfloat16), "roll").astype(jnp.float32),
         lax.psum(shares[2].astype(jnp.bfloat16), "roll").astype(jnp.float32),
         lax.psum(shares[3].astype(jnp.bfloat16), "roll").astype(jnp.float32),

time: 690 us -> 704 us (1.020)
    all_gather x0 -> x1, waiting for transfers between devices: none -> 17.3 us  [local(): lax.all_gather(shares[0].astype(jnp.bfloat16), 'roll')]
    psum x1, waiting for transfers between devices: 45.4 us -> 36.1 us  [local(): lax.psum(shares[1].astype(jnp.bfloat16), 'roll').astype(jnp.float32)]
    unnamed x87 -> x85, local copies, waits for them, and re-layouts: 51.6 us -> 50.9 us
  transfers between devices with their start and end apart: 9 -> 10, of which waited for: 8 -> 8; matrix products, arithmetic and copies ran while one was open for 27% -> 28% of each run, Pallas kernels for 0% -> 0%
where the time goes in v1:
time: 704 us; the launch traced here: 698 us
  waiting for transfers between devices  353 us (50%)
  local copies, waits for them, and re-layouts  162 us (23%)
  matrix products  71.9 us (10%)
  starting transfers between devices  35.7 us (5%)
  blocking collectives  32.7 us (5%)
  other arithmetic  27.1 us (4%)
  between operations  15.1 us (2%)
    reduce_scatter x1, waiting for transfers between devices, local(): lax.psum_scatter(partials[1], 'tm', scatter_dimension=0, tiled=True)  91.9 us
    reduce_scatter x1, waiting for transfers between devices, local(): lax.psum_scatter(partials[2], 'tm', scatter_dimension=0, tiled=True)  91.7 us
    all_to_all x1, waiting for transfers between devices, local(): lax.all_to_all(slot_grad, 'tm', split_axis=0, concat_axis=0, tiled=True)  52.4 us
    unnamed x85, local copies, waits for them, and re-layouts  50.9 us
    ppermute x2, waiting for transfers between devices, from_behind(): return lax.ppermute(block, axis, route)  41.4 us
    psum x1, waiting for transfers between devices, local(): lax.psum(shares[1].astype(jnp.bfloat16), 'roll').astype(jnp.float32)  36.1 us
    all_gather x1, blocking collectives, local(): all_lists = lax.all_gather(recalled, 'tm', axis=0, tiled=True)  32.7 us
    all_to_all x1, starting transfers between devices, local(): lax.all_to_all(slot_grad, 'tm', split_axis=0, concat_axis=0, tiled=True)  23.1 us
  transfers between devices with their start and end apart: 10, of which 8 were waited for; matrix products, arithmetic and copies ran while one was open for 28% of the time, Pallas kernels for 0%

profile of v1, /device:TPU:0, one launch (start us, length us, event | category | flops | bytes accessed | tf_op | source)
XLA Modules:
  0.0 697.9 jit_solution(13933031880876175388)
XLA Ops:
  7.2 32.7 %all-gather = s32[1,64,8]{2,1,0:T(8,128)S(1)} all-gather(s32[1,8,8]{2,1,0:T(8,128)} %param.9), channel_id=2, replica_groups=mesh['tm'=8,'roll'=4] {'tm'}, dimensions={1}, use_global_device_ids=true | all-gather | bytes 2304 | tf_op jit(solution)/shard_map/all_gather | solution.py:123
  50.9 5.6 all-to-all-start
  70.3 19.8 %collective-permute-done = bf16[4,32,2048]{2,1,0:T(8,128)(2,1)} collective-permute-done((bf16[4,32,2048]{2,1,0:T(8,128)(2,1)}, bf16[4,32,2048]{2,1,0:T(8,128)(2,1)}, u32[]{:S(2)}, u32[]{:S(2)}) %collective-permute-start) | collective-permute-done | bytes 524320 | tf_op jit(solution)/shard_map/ppermute | solution.py:17
  99.1 22.1 %all-to-all-done = bf16[8,3,32,2048]{3,2,1,0:T(8,128)(2,1)} async-done(((bf16[8,3,32,2048]{3,2,1,0:T(8,128)(2,1)}), bf16[8,3,32,2048]{3,2,1,0:T(8,128)(2,1)}, u32[]{:S(2)}, u32[]{:S(2)}) %all-to-all-start) | async-done | bytes 3145760 | tf_op jit(solution)/shard_map/all_to_all | solution.py:159
  131.7 4.9 constant_dynamic-update-slice_fusion.2
  136.7 4.9 copy.178
  144.3 5.5 copy.177
  168.1 5.8 fusion.42
  174.9 7.0 convolution_bitcast_fusion
  181.9 17.5 %copy.149 = f32[8,416,8,128]{3,2,1,0:T(8,128)} copy(f32[8,416,8,128]{3,1,2,0:T(8,128)} %convolution_bitcast_fusion) | data formatting | bytes 27262976 | tf_op jit(solution)/shard_map/fhqk,fqhe->fkhe/transpose | solution.py:63
  199.4 15.8 %reshape.193 = f32[8,13,32,1024]{3,2,1,0:T(8,128)} reshape(f32[8,416,8,128]{3,2,1,0:T(8,128)} %copy.149) | data formatting | bytes 27262976 | tf_op jit(solution)/shard_map/reshape | solution.py:69
  219.4 5.0 copy.184
  228.3 6.3 multiply_bitcast_fusion
  234.6 17.5 %copy.142 = f32[8,416,8,128]{3,2,1,0:T(8,128)} copy(f32[8,416,8,128]{3,1,2,0:T(8,128)} %multiply_bitcast_fusion) | data formatting | bytes 27262976 | tf_op jit(solution)/shard_map/mul | solution.py:60
  252.2 16.0 %reshape.192 = f32[8,13,32,1024]{3,2,1,0:T(8,128)} reshape(f32[8,416,8,128]{3,2,1,0:T(8,128)} %copy.142) | data formatting | bytes 27262976 | tf_op jit(solution)/shard_map/reshape | solution.py:68
  275.9 5.0 copy.182
  286.2 23.1 %all-to-all-start.1 = ((bf16[8,3,32,2048]{3,2,1,0:T(8,128)(2,1)}), bf16[8,3,32,2048]{3,2,1,0:T(8,128)(2,1)}, u32[]{:S(2)}, u32[]{:S(2)}) async-start(bf16[8,3,32,2048]{3,2,1,0:T(8,128)(2,1)} %pad_maximum_fusion.1), calls=%async_computation.1 | async-start | bytes 6291456 | tf_op jit(solution)/shard_map/all_to_all | solution.py:191
  327.4 21.7 %collective-permute-done.1 = bf16[4,32,2048]{2,0,1:T(4,128)(2,1)S(1)} collective-permute-done((bf16[4,32,2048]{2,0,1:T(4,128)(2,1)S(1)}, bf16[4,32,2048]{2,0,1:T(4,128)(2,1)S(1)}, u32[]{:S(2)}, u32[]{:S(2)}) %collective-permute-start.1) | collective-permute-done | bytes 524320 | tf_op jit(solution)/shard_map/ppermute | solution.py:17
  349.4 52.4 %all-to-all-done.1 = bf16[8,3,32,2048]{3,2,1,0:T(8,128)(2,1)} async-done(((bf16[8,3,32,2048]{3,2,1,0:T(8,128)(2,1)}), bf16[8,3,32,2048]{3,2,1,0:T(8,128)(2,1)}, u32[]{:S(2)}, u32[]{:S(2)}) %all-to-all-start.1) | async-done | bytes 3145760 | tf_op jit(solution)/shard_map/all_to_all | solution.py:191
  405.8 5.2 reshape.198
  431.5 91.7 %reduce-scatter.9.cloned.1.call-done = bf16[256,1024]{0,1:T(8,128)(2,1)} async-done(((bf16[2048,1024]{0,1:T(8,128)(2,1)}), bf16[256,1024]{0,1:T(8,128)(2,1)}) %reduce-scatter.9.cloned.1.call-update) | async-done | bytes 524304 | tf_op jit(solution)/shard_map/reduce_scatter | solution.py:223
  523.1 91.9 %reduce-scatter.7.cloned.1.call-done = bf16[256,1024]{0,1:T(8,128)(2,1)} async-done(((bf16[2048,1024]{0,1:T(8,128)(2,1)}), bf16[256,1024]{0,1:T(8,128)(2,1)}) %reduce-scatter.7.cloned.1.call-update) | async-done | bytes 524304 | tf_op jit(solution)/shard_map/reduce_scatter | solution.py:222
  621.6 17.3 %all-gather.4.cloned.1.call-done = bf16[1024,1024]{0,1:T(8,128)(2,1)} async-done(((bf16[256,1024]{0,1:T(8,128)(2,1)}), bf16[1024,1024]{0,1:T(8,128)(2,1)}) %all-gather.4.cloned.1.call-update) | async-done | bytes 2097168 | tf_op jit(solution)/shard_map/all_gather | solution.py:227
  648.1 36.1 %all-reduce.14.cloned.1.call-done = (bf16[256,1024]{0,1:T(8,128)(2,1)}, bf16[256,1024]{0,1:T(8,128)(2,1)}, bf16[128,2048]{1,0:T(8,128)(2,1)}) async-done(((bf16[256,1024]{0,1:T(8,128)(2,1)}, bf16[256,1024]{0,1:T(8,128)(2,1)}, bf16[128,2048]{1,0:T(8,128)(2,1)}), (bf16[256,1024]{0,1:T(8,128)(2,1)}, bf16[256,1024]{0,1:T(8,128)(2,1)}, bf16[128,2048]{1,0:T(8,128)(2,1)})) %all-reduce.14.cloned.1.call-update) | async-done | bytes 1572880 | tf_op jit(solution)/shard_map/psum | solution.py:228
  (190 shorter events, 151.9 us)
Async XLA Ops:
  7.2 33.4 %copy-start = (bf16[1,8,32,2048]{3,2,1,0:T(8,128)(2,1)S(1)}, bf16[1,8,32,2048]{3,2,1,0:T(8,128)(2,1)}, u32[]{:S(2)}) copy-start(bf16[1,8,32,2048]{3,2,1,0:T(8,128)(2,1)} %param.7) | copy-start | bytes 3145732
  40.3 7.2 %copy-start.25 = (pred[8,8]{0,1:T(8,128)(4,1)}, pred[8,8]{0,1:T(8,128)(4,1)S(1)}, u32[]{:S(2)}) copy-start(pred[8,8]{0,1:T(8,128)(4,1)S(1)} %copy.119) | copy-start | bytes 196
  40.6 6.9 copy-start.23
  50.9 11.4 %copy-start.22 = (s32[1,8,8]{2,1,0:T(8,128)S(1)}, s32[1,8,8]{2,1,0:T(8,128)}, u32[]{:S(2)}) copy-start(s32[1,8,8]{2,1,0:T(8,128)} %param.9) | copy-start | bytes 772
  50.9 70.3 %all-to-all-start = ((bf16[8,3,32,2048]{3,2,1,0:T(8,128)(2,1)}), bf16[8,3,32,2048]{3,2,1,0:T(8,128)(2,1)}, u32[]{:S(2)}, u32[]{:S(2)}) async-start(bf16[8,3,32,2048]{3,2,1,0:T(8,128)(2,1)} %pad_maximum_fusion), calls=%async_computation | async-start | bytes 6291456 | tf_op jit(solution)/shard_map/all_to_all | solution.py:159
  56.6 366.7 %reduce-scatter.5.cloned.1.call-start = ((), (), s32[]{:S(2)}) async-start(), calls=%async_computation.6 | async-start | bytes 4718592 | tf_op jit(solution)/shard_map/reduce_scatter | solution.py:221
  57.5 32.6 %collective-permute-start = (bf16[4,32,2048]{2,1,0:T(8,128)(2,1)}, bf16[4,32,2048]{2,1,0:T(8,128)(2,1)}, u32[]{:S(2)}, u32[]{:S(2)}) collective-permute-start(bf16[4,32,2048]{2,1,0:T(8,128)(2,1)} %pad_maximum_fusion.4), channel_id=1, source_target_pairs={{0,4},{4,8},{8,12},{12,16},{16,20},{20,24},{24,28},{1,5},{5,9},{9,... | collective-permute-start | bytes 1572872 | tf_op jit(solution)/shard_map/ppermute | solution.py:17
  68.0 81.9 %copy-start.10 = (bf16[32,8,8,128]{3,2,1,0:T(8,128)(2,1)}, bf16[32,8,8,128]{3,2,1,0:T(8,128)(2,1)S(1)}, u32[]{:S(2)}) copy-start(bf16[32,8,8,128]{3,2,1,0:T(8,128)(2,1)S(1)} %copy.176) | copy-start | bytes 1572868
  136.7 4.9 copy-start.1
  141.6 13.5 %copy-start.4 = (bf16[416,8,8,128]{3,2,1,0:T(8,128)(2,1)}, bf16[416,8,8,128]{3,2,1,0:T(8,128)(2,1)S(1)}, u32[]{:S(2)}) copy-start(bf16[416,8,8,128]{3,2,1,0:T(8,128)(2,1)S(1)} %copy.178) | copy-start | bytes 20447236
  168.0 263.5 %reduce-scatter.11.cloned.1.call-start = ((), (), s32[]{:S(2)}) async-start(), calls=%async_computation.9 | async-start | bytes 4718592 | tf_op jit(solution)/shard_map/reduce_scatter | solution.py:224
  168.0 6.9 copy-start.3
  168.1 6.9 copy-start.19
  252.1 16.1 %copy-start.15 = (bf16[8,32,8,128]{3,2,1,0:T(8,128)(2,1)S(1)}, bf16[8,32,8,128]{3,2,1,0:T(8,128)(2,1)}, u32[]{:S(2)}) copy-start(bf16[8,32,8,128]{3,2,1,0:T(8,128)(2,1)} %copy.136) | copy-start | bytes 1572868
  252.2 16.1 %copy-start.21 = (bf16[1,8,32,2048]{3,2,1,0:T(8,128)(2,1)S(1)}, bf16[1,8,32,2048]{3,2,1,0:T(8,128)(2,1)}, u32[]{:S(2)}) copy-start(bf16[1,8,32,2048]{3,2,1,0:T(8,128)(2,1)} %param.8) | copy-start | bytes 3145732
  286.2 115.6 %all-to-all-start.1 = ((bf16[8,3,32,2048]{3,2,1,0:T(8,128)(2,1)}), bf16[8,3,32,2048]{3,2,1,0:T(8,128)(2,1)}, u32[]{:S(2)}, u32[]{:S(2)}) async-start(bf16[8,3,32,2048]{3,2,1,0:T(8,128)(2,1)} %pad_maximum_fusion.1), calls=%async_computation.1 | async-start | bytes 6291456 | tf_op jit(solution)/shard_map/all_to_all | solution.py:191
  309.3 213.9 %reduce-scatter.9.cloned.1.call-start = ((), (), s32[]{:S(2)}) async-start(), calls=%async_computation.8 | async-start | bytes 4718592 | tf_op jit(solution)/shard_map/reduce_scatter | solution.py:223
  325.9 23.2 %collective-permute-start.1 = (bf16[4,32,2048]{2,0,1:T(4,128)(2,1)S(1)}, bf16[4,32,2048]{2,0,1:T(4,128)(2,1)S(1)}, u32[]{:S(2)}, u32[]{:S(2)}) collective-permute-start(bf16[4,32,2048]{2,0,1:T(4,128)(2,1)S(1)} %pad_maximum_fusion.5), channel_id=1, source_target_pairs={{4,0},{8,4},{12,8},{16,12},{20,16},{24,20},{28,24},{5,1},{9,5},{13... | collective-permute-start | bytes 1572872 | tf_op jit(solution)/shard_map/ppermute | solution.py:17
  405.8 5.2 copy-start.24
  405.8 5.2 copy-start.26
  419.6 195.5 %reduce-scatter.7.cloned.1.call-start = ((), (), s32[]{:S(2)}) async-start(), calls=%async_computation.7 | async-start | bytes 4718592 | tf_op jit(solution)/shard_map/reduce_scatter | solution.py:222
  423.2 5.6 copy-start.14
  423.2 215.7 %all-gather.4.cloned.1.call-start = ((), (), s32[]{:S(2)}) async-start(), calls=%async_computation.10 | async-start | bytes 2621440 | tf_op jit(solution)/shard_map/all_gather | solution.py:227
  423.8 260.4 %all-reduce.14.cloned.1.call-start = ((), (), s32[]{:S(2)}) async-start(), calls=%async_computation.11 | async-start | bytes 3145728 | tf_op jit(solution)/shard_map/psum | solution.py:228
  (16 other events, 45.7 us)
Sparse Core Ops, SparseCore 0:
  168.1 106.9 reduce-scatter.4
  278.7 152.0 reduce-scatter.10
  434.5 88.6 reduce-scatter.8
  526.6 88.3 reduce-scatter.6
  616.4 22.4 all-gather.3
  641.3 42.8 all-reduce.13
